TPU v7x, 512 devices: a whole 4x4x16 slice. The times are simulated.
512 devices in a mesh: ta: 8 (over y, z_hi), ha: 4 (over x), wa: 16 (over z_lo, core).
Axes of the slice: x: 4, y: 4, z: 16 (z_hi: 2, z_lo: 8; z = z_hi * 8 + z_lo), core: 2. Of those that a mesh axis runs over, the one named last changes fastest.
Arguments:
- features: bfloat16 [16, 64, 256, 256], P('ta', 'ha', 'wa'), may hold values from -6 to 6
- conv_weight: bfloat16 [6912, 256], P('wa'), may hold values from -0.078125 to 0.078125
- down_weight: bfloat16 [2, 2, 256, 256], replicated, may hold values from -0.1875 to 0.1875
- grad_out: bfloat16 [16, 32, 128, 256], P('ta', 'ha', 'wa'), may hold values from -6 to 6
- crop_grad: bfloat16 [32768, 8, 8, 256], P(('ta', 'ha', 'wa')), may hold values from -6 to 6
- crop_owner: int32 [32768, 1], P(('ta', 'ha', 'wa')), may hold values from 0 to 63; in each aligned block of 64 rows (0 to 63, 64 to 127, ...) at most 2 rows name the same one
- crop_frame: int32 [32768], P(('ta', 'ha', 'wa')), may hold values from 0 to 1
- crop_row: int32 [32768], P(('ta', 'ha', 'wa')), may hold values from 0 to 8
- crop_col: int32 [32768], P(('ta', 'ha', 'wa')), may hold values from 0 to 8
- crop_valid: int32 [32768], P(('ta', 'ha', 'wa')), may hold values 0 or 1
Outputs:
- reduced: bfloat16 [16, 32, 128, 256], P('ta', 'ha', 'wa')
- grad_in: bfloat16 [16, 64, 256, 256], P('ta', 'ha', 'wa')
Inputs may be any that keep to these rules, and one draw needn't show every extreme that they name: `crop_owner`: among one device's 64 crops at most 2 name the same owner, a bound that some block reaches; the owner is the tile of the same time slab whose height index is the value divided by the number of width tiles and whose width index is the remainder. `crop_frame`: frame of the crop within the time slab of the device that holds it. `crop_valid`: padding crops carry gradients that are ignored.
All inputs are finite; a program needn't handle non-finite values. No bound on the sum of `crop_valid` on one device may be relied on, other than what follows from the above.
Results may differ from a plain program's by a relative error of at most 0.0049.
Values may be sent and summed in bfloat16 or wider, within the bound.
A program may use at most 64 MiB of HBM per device.

v0:
```python
import jax
import jax.numpy as jnp
from jax import lax
from jax.sharding import PartitionSpec as P

CH = 8
CW = 8
CAP = 2


def extended(block, sides, width):
    for axis, dim in sides:
        count = lax.axis_size(axis)
        forward = [(i, i + 1) for i in range(count - 1)]
        backward = [(target, source) for source, target in forward]
        low = lax.ppermute(
            lax.slice_in_dim(block, block.shape[dim] - width, None, axis=dim), axis, forward
        )
        high = lax.ppermute(lax.slice_in_dim(block, 0, width, axis=dim), axis, backward)
        block = jnp.concatenate([low, block, high], axis=dim)
    return block


def from_behind(value, axis, steps):
    count = lax.axis_size(axis)
    first, last = (max(0, -steps), min(count, count - steps))
    return lax.ppermute(value, axis, [(source, source + steps) for source in range(first, last)])


def convolve(padded, kernel_taps, frames, rows, cols):
    width = kernel_taps.shape[-1]
    summed = jnp.zeros((frames * rows * cols, width), jnp.float32)
    for frame_off in range(3):
        windows = []
        for row_off in range(3):
            for col_off in range(3):
                windows.append(
                    padded[
                        frame_off : frame_off + frames,
                        row_off : row_off + rows,
                        col_off : col_off + cols,
                        :,
                    ]
                )
        stacked = jnp.concatenate(windows, -1).reshape(frames * rows * cols, 9 * width)
        tap_block = kernel_taps[frame_off * 9 : (frame_off + 1) * 9].reshape(9 * width, width)
        summed = summed + jnp.dot(stacked, tap_block, preferred_element_type=jnp.float32)
    return summed.reshape(frames, rows, cols, width)


def widen(block):
    return extended(block, (("ha", 1), ("wa", 2)), 1)


def per_device(
    features,
    conv_weight,
    down_weight,
    grad_out,
    crop_grad,
    crop_owner,
    crop_frame,
    crop_row,
    crop_col,
    crop_valid,
):
    frames, rows, cols, width = features.shape
    height_tiles = lax.axis_size("ha")
    width_tiles = lax.axis_size("wa")
    owners_all = height_tiles * width_tiles
    slots_all = owners_all * CAP
    count = crop_owner.shape[0]
    owner_id = crop_owner[:, 0]
    onehot = (owner_id[:, None] == jnp.arange(owners_all, dtype=jnp.int32)[None, :]).astype(
        jnp.int32
    )
    earlier = jnp.cumsum(onehot, 0) - onehot
    slot_rank = jnp.sum(earlier * onehot, 1)
    target = owner_id * CAP + slot_rank
    placing = target[:, None] == jnp.arange(slots_all, dtype=jnp.int32)[None, :]
    weighted = crop_grad * crop_valid.astype(jnp.bfloat16)[:, None, None, None]
    packed = jnp.dot(
        placing.astype(jnp.bfloat16).T,
        weighted.reshape(count, -1),
        preferred_element_type=jnp.float32,
    ).astype(jnp.bfloat16)
    place_meta = jnp.stack([crop_frame, crop_row, crop_col], 1)
    meta_sent = jnp.sum(placing.astype(jnp.int32)[:, :, None] * place_meta[:, None, :], 0)
    received, got_meta = (
        lax.all_to_all(packed, ("ha", "wa"), split_axis=0, concat_axis=0, tiled=True),
        lax.all_to_all(meta_sent, ("ha", "wa"), split_axis=0, concat_axis=0, tiled=True),
    )
    row_steps = jnp.arange(CH, dtype=jnp.int32)
    col_steps = jnp.arange(CW, dtype=jnp.int32)
    cell_index = (
        (got_meta[:, 0, None, None] * rows + got_meta[:, 1, None, None] + row_steps[None, :, None])
        * cols
        + got_meta[:, 2, None, None]
        + col_steps[None, None, :]
    )
    crop_terms = (
        jnp.zeros((frames * rows * cols, width), jnp.float32)
        .at[cell_index.reshape(-1)]
        .add(received.reshape(-1, width).astype(jnp.float32))
    )
    gathered = lax.all_gather(conv_weight, "wa", axis=0, tiled=True)
    kernel_taps = gathered.reshape(27, width, width)
    past = from_behind(features, "ta", 1)
    padded = widen(jnp.concatenate([past, features], 0))
    preact = convolve(padded, kernel_taps, frames, rows, cols)
    sigmoid_h = jax.nn.sigmoid(preact)
    section_out = (features.astype(jnp.float32) + preact * sigmoid_h).astype(jnp.bfloat16)
    down_mat = down_weight.reshape(4 * width, width)
    pooled = (
        section_out.reshape(frames, rows // 2, 2, cols // 2, 2, width)
        .transpose(0, 1, 3, 2, 4, 5)
        .reshape(-1, 4 * width)
    )
    reduced = (
        jnp.dot(pooled, down_mat, preferred_element_type=jnp.float32)
        .astype(jnp.bfloat16)
        .reshape(frames, rows // 2, cols // 2, width)
    )
    spread = jnp.dot(grad_out.reshape(-1, width), down_mat.T, preferred_element_type=jnp.float32)
    spread = (
        spread.reshape(frames, rows // 2, cols // 2, 2, 2, width)
        .transpose(0, 1, 3, 2, 4, 5)
        .reshape(frames, rows, cols, width)
    )
    grad_pre = (spread * sigmoid_h * (1.0 + preact * (1.0 - sigmoid_h))).astype(jnp.bfloat16)
    flipped = jnp.transpose(kernel_taps[::-1], (0, 2, 1))
    future = from_behind(grad_pre, "ta", -1)
    back_pad = widen(jnp.concatenate([grad_pre, future], 0))
    through = convolve(back_pad, flipped, frames, rows, cols)
    grad_in = (spread + through + crop_terms.reshape(frames, rows, cols, width)).astype(
        jnp.bfloat16
    )
    return (reduced, grad_in)


def solution(mesh):
    in_specs = (
        P("ta", "ha", "wa", None),
        P("wa", None),
        P(),
        P("ta", "ha", "wa", None),
        P(("ta", "ha", "wa"), None, None, None),
        P(("ta", "ha", "wa"), None),
        P(("ta", "ha", "wa")),
        P(("ta", "ha", "wa")),
        P(("ta", "ha", "wa")),
        P(("ta", "ha", "wa")),
    )
    out_specs = (P("ta", "ha", "wa", None), P("ta", "ha", "wa", None))
    return jax.shard_map(
        per_device, mesh=mesh, in_specs=in_specs, out_specs=out_specs, check_vma=False
    )
```

profile of v0, /device:TPU:27, one launch (start us, length us, event | category | flops | bytes accessed | tf_op | source)
XLA Modules:
  0.0 448.2 jit_solution(8883349491360563896)
XLA Ops:
  7.2 0.8 fusion.23
  8.1 0.8 select_reduce_fusion
  11.2 16.4 %all-to-all-start = ((s32[64,2,3]{2,1,0:T(2,128)}), s32[64,2,3]{2,1,0:T(2,128)S(1)}, u32[]{:S(2)}, u32[]{:S(2)}) async-start(s32[64,2,3]{2,1,0:T(2,128)} %bitcast.28), calls=%async_computation | async-start | bytes 131072 | tf_op jit(solution)/shard_map/all_to_all | solution.py:91
  28.3 1.8 broadcast_multiply_fusion
  30.1 1.3 copy.92
  31.4 3.3 convolution_convert_fusion
  34.7 7.7 %all_to_all.17 = bf16[64,2,16384]{2,1,0:T(2,128)(2,1)} reshape(bf16[128,16384]{1,0:T(8,128)(2,1)} %convolution_convert_fusion) | data formatting | bytes 8388608 | tf_op jit(solution)/shard_map/all_to_all | solution.py:90
  42.4 13.4 %all-to-all-start.1 = ((bf16[64,2,16384]{2,1,0:T(2,128)(2,1)}), bf16[64,2,16384]{2,1,0:T(2,128)(2,1)}, u32[]{:S(2)}, u32[]{:S(2)}) async-start(bf16[64,2,16384]{2,1,0:T(2,128)(2,1)} %all_to_all.17), calls=%async_computation.1 | async-start | bytes 8388608 | tf_op jit(solution)/shard_map/all_to_all | solution.py:90
  56.5 7.9 %collective-permute-start = (bf16[2,16,16,256]{3,2,1,0:T(8,128)(2,1)S(1)}, bf16[2,16,16,256]{3,2,1,0:T(8,128)(2,1)S(1)}, u32[]{:S(2)}, u32[]{:S(2)}) collective-permute-start(bf16[2,16,16,256]{3,2,1,0:T(8,128)(2,1)S(1)} %copy-done.3), channel_id=1, source_target_pairs={{0,64},{64,128},{128,192},{192,256},{256,320},{320,384},{384,448},... | collective-permute-start | bytes 786440 | tf_op jit(solution)/shard_map/ppermute | solution.py:27
  65.7 109.0 %collective-permute-done = bf16[2,16,16,256]{3,2,1,0:T(8,128)(2,1)S(1)} collective-permute-done((bf16[2,16,16,256]{3,2,1,0:T(8,128)(2,1)S(1)}, bf16[2,16,16,256]{3,2,1,0:T(8,128)(2,1)S(1)}, u32[]{:S(2)}, u32[]{:S(2)}) %collective-permute-start) | collective-permute-done | bytes 262176 | tf_op jit(solution)/shard_map/ppermute | solution.py:27
  174.7 3.2 collective-permute-start.1
  177.9 2.1 collective-permute-start.2
  180.5 2.5 collective-permute-done.2
  183.2 1.9 collective-permute-start.3
  185.1 3.1 collective-permute-start.4
  188.3 4.0 collective-permute-done.4
  192.9 1.0 slice_dynamic-update-slice_fusion.29
  193.9 1.0 fusion.18
  194.9 1.1 slice_dynamic-update-slice_fusion.28
  196.0 1.1 slice_dynamic-update-slice_fusion.27
  197.1 0.8 constant_dynamic-update-slice_fusion.3
  197.9 0.9 slice_dynamic-update-slice_fusion.33
  198.8 1.1 slice_dynamic-update-slice_fusion.26
  200.0 1.0 slice_dynamic-update-slice_fusion.25
  201.0 1.0 fusion.17
  202.0 1.2 slice_dynamic-update-slice_fusion.24
  203.2 43.4 %all-gather.2.cloned.1.call-done = bf16[6912,256]{1,0:T(8,128)(2,1)} async-done(((bf16[432,256]{1,0:T(8,128)(2,1)}), bf16[6912,256]{1,0:T(8,128)(2,1)}) %all-gather.2.cloned.1.call-update) | async-done | bytes 3538960 | tf_op jit(solution)/shard_map/all_gather | solution.py:106
  246.5 2.9 fusion.2
  249.6 2.4 convolution_add_fusion.3
  252.0 2.4 convolution_add_fusion.2
  254.8 13.7 %collective-permute-start.5 = (bf16[2,16,16,256]{3,2,1,0:T(8,128)(2,1)S(1)}, bf16[2,16,16,256]{3,2,1,0:T(8,128)(2,1)S(1)}, u32[]{:S(2)}, u32[]{:S(2)}) collective-permute-start(bf16[2,16,16,256]{3,2,1,0:T(8,128)(2,1)S(1)} %get-tuple-element.75), channel_id=1, source_target_pairs={{64,0},{128,64},{192,128},{256,192},{320,256},{384,320},{448,384},... | collective-permute-start | bytes 786440 | tf_op jit(solution)/shard_map/ppermute | solution.py:27
  269.0 2.4 reverse_bitcast_fusion
  271.4 1.7 fusion.26
  273.1 4.5 %collective-permute-start.6 = (bf16[4,1,16,256]{3,2,1,0:T(8,128)(2,1)S(1)}, bf16[4,1,16,256]{3,2,1,0:T(8,128)(2,1)S(1)}, u32[]{:S(2)}, u32[]{:S(2)}) collective-permute-start(bf16[4,1,16,256]{3,2,1,0:T(8,128)(2,1)S(1)} %get-tuple-element.73), channel_id=1, source_target_pairs={{0,16},{16,32},{32,48},{1,17},{17,33},{33,49},{2,18},{18,34},{34,5... | collective-permute-start | bytes 98312 | tf_op jit(solution)/shard_map/ppermute | solution.py:16
  277.7 1.9 collective-permute-start.7
  279.6 0.9 convolution_convert_fusion.1
  280.5 2.4 copy.76
  282.9 1.5 copy.77
  284.4 1.6 copy.78
  286.1 90.1 %collective-permute-start.8 = (bf16[4,18,1,256]{3,2,1,0:T(2,128)(2,1)S(1)}, bf16[4,18,1,256]{3,2,1,0:T(2,128)(2,1)S(1)}, u32[]{:S(2)}, u32[]{:S(2)}) collective-permute-start(bf16[4,18,1,256]{3,2,1,0:T(2,128)(2,1)S(1)} %get-tuple-element.54), channel_id=1, source_target_pairs={{0,1},{1,2},{2,3},{3,4},{4,5},{5,6},{6,7},{7,8},{8,9},{9,10},{10,1... | collective-permute-start | bytes 110600 | tf_op jit(solution)/shard_map/ppermute | solution.py:16
  376.2 1.9 collective-permute-start.9
  378.3 3.6 collective-permute-done.9
  383.5 0.9 copy-done.4
  385.2 0.8 convolution_add_fusion.1
  386.0 0.8 convolution_add_fusion
  386.8 8.2 %reshape.228 = f32[8192,256]{1,0:T(8,128)} reshape(bf16[64,2,16384]{2,1,0:T(2,128)(2,1)} %all-to-all-done.1) | data formatting | bytes 12582912 | tf_op jit(solution)/shard_map/convert_element_type | solution.py:104
  395.0 44.7 %scatter_custom_fusion = f32[512,256]{1,0:T(8,128)S(1)} fusion(s32[8192]{0:T(1024)S(1)} %bitcast.83, f32[8192,256]{1,0:T(8,128)} %reshape.228, f32[]{:T(128)} %constant.7.clone.1), kind=kCustom, calls=%fused_computation.96 | custom fusion | flops 2097152 | bytes 524800 | tf_op jit(solution)/shard_map/scatter-add | solution.py:104
  439.7 0.9 fusion.5
  (64 shorter events, 10.4 us)
Async XLA Ops:
  7.2 57.3 %copy-start = (bf16[2,2,256,256]{3,2,1,0:T(8,128)(2,1)S(1)}, bf16[2,2,256,256]{3,2,1,0:T(8,128)(2,1)}, u32[]{:S(2)}) copy-start(bf16[2,2,256,256]{3,2,1,0:T(8,128)(2,1)} %param.12) | copy-start | bytes 1572868
  11.2 31.2 %all-to-all-start = ((s32[64,2,3]{2,1,0:T(2,128)}), s32[64,2,3]{2,1,0:T(2,128)S(1)}, u32[]{:S(2)}, u32[]{:S(2)}) async-start(s32[64,2,3]{2,1,0:T(2,128)} %bitcast.28), calls=%async_computation | async-start | bytes 131072 | tf_op jit(solution)/shard_map/all_to_all | solution.py:91
  42.4 14.1 %copy-start.3 = (bf16[2,16,16,256]{3,2,1,0:T(8,128)(2,1)S(1)}, bf16[2,16,16,256]{3,2,1,0:T(8,128)(2,1)}, u32[]{:S(2)}) copy-start(bf16[2,16,16,256]{3,2,1,0:T(8,128)(2,1)} %param.10) | copy-start | bytes 786436
  42.4 22.1 %copy-start.5 = (bf16[2,8,8,256]{3,2,1,0:T(8,128)(2,1)S(1)}, bf16[2,8,8,256]{3,2,1,0:T(8,128)(2,1)}, u32[]{:S(2)}) copy-start(bf16[2,8,8,256]{3,2,1,0:T(8,128)(2,1)} %param.13) | copy-start | bytes 196612
  42.4 344.4 %all-to-all-start.1 = ((bf16[64,2,16384]{2,1,0:T(2,128)(2,1)}), bf16[64,2,16384]{2,1,0:T(2,128)(2,1)}, u32[]{:S(2)}, u32[]{:S(2)}) async-start(bf16[64,2,16384]{2,1,0:T(2,128)(2,1)} %all_to_all.17), calls=%async_computation.1 | async-start | bytes 8388608 | tf_op jit(solution)/shard_map/all_to_all | solution.py:90
  55.8 190.8 %all-gather.2.cloned.1.call-start = ((), (), s32[]{:S(2)}) async-start(), calls=%async_computation.2 | async-start | bytes 3760128 | tf_op jit(solution)/shard_map/all_gather | solution.py:106
  56.5 118.1 %collective-permute-start = (bf16[2,16,16,256]{3,2,1,0:T(8,128)(2,1)S(1)}, bf16[2,16,16,256]{3,2,1,0:T(8,128)(2,1)S(1)}, u32[]{:S(2)}, u32[]{:S(2)}) collective-permute-start(bf16[2,16,16,256]{3,2,1,0:T(8,128)(2,1)S(1)} %copy-done.3), channel_id=1, source_target_pairs={{0,64},{64,128},{128,192},{192,256},{256,320},{320,384},{384,448},... | collective-permute-start | bytes 786440 | tf_op jit(solution)/shard_map/ppermute | solution.py:27
  174.7 5.8 %collective-permute-start.1 = (bf16[4,1,16,256]{3,2,1,0:T(8,128)(2,1)S(1)}, bf16[4,1,16,256]{3,2,1,0:T(8,128)(2,1)S(1)}, u32[]{:S(2)}, u32[]{:S(2)}) collective-permute-start(bf16[4,1,16,256]{3,2,1,0:T(8,128)(2,1)S(1)} %get-tuple-element.77), channel_id=1, source_target_pairs={{0,16},{16,32},{32,48},{1,17},{17,33},{33,49},{2,18},{18,34},{34,5... | collective-permute-start | bytes 98312 | tf_op jit(solution)/shard_map/ppermute | solution.py:16
  177.9 5.2 %collective-permute-start.2 = (bf16[4,1,16,256]{3,2,1,0:T(8,128)(2,1)S(1)}, bf16[4,1,16,256]{3,2,1,0:T(8,128)(2,1)S(1)}, u32[]{:S(2)}, u32[]{:S(2)}) collective-permute-start(bf16[4,1,16,256]{3,2,1,0:T(8,128)(2,1)S(1)} %get-tuple-element.78), channel_id=1, source_target_pairs={{16,0},{32,16},{48,32},{17,1},{33,17},{49,33},{18,2},{34,18},{50,3... | collective-permute-start | bytes 98312 | tf_op jit(solution)/shard_map/ppermute | solution.py:19
  183.2 5.1 %collective-permute-start.3 = (bf16[4,18,1,256]{3,2,1,0:T(2,128)(2,1)S(1)}, bf16[4,18,1,256]{3,2,1,0:T(2,128)(2,1)S(1)}, u32[]{:S(2)}, u32[]{:S(2)}) collective-permute-start(bf16[4,18,1,256]{3,2,1,0:T(2,128)(2,1)S(1)} %get-tuple-element.58), channel_id=1, source_target_pairs={{0,1},{1,2},{2,3},{3,4},{4,5},{5,6},{6,7},{7,8},{8,9},{9,10},{10,1... | collective-permute-start | bytes 110600 | tf_op jit(solution)/shard_map/ppermute | solution.py:16
  185.1 7.2 %collective-permute-start.4 = (bf16[4,18,1,256]{3,2,1,0:T(2,128)(2,1)S(1)}, bf16[4,18,1,256]{3,2,1,0:T(2,128)(2,1)S(1)}, u32[]{:S(2)}, u32[]{:S(2)}) collective-permute-start(bf16[4,18,1,256]{3,2,1,0:T(2,128)(2,1)S(1)} %get-tuple-element.57), channel_id=1, source_target_pairs={{1,0},{2,1},{3,2},{4,3},{5,4},{6,5},{7,6},{8,7},{9,8},{10,9},{11,1... | collective-permute-start | bytes 110600 | tf_op jit(solution)/shard_map/ppermute | solution.py:19
  246.5 3.1 copy-start.2
  254.8 18.3 %collective-permute-start.5 = (bf16[2,16,16,256]{3,2,1,0:T(8,128)(2,1)S(1)}, bf16[2,16,16,256]{3,2,1,0:T(8,128)(2,1)S(1)}, u32[]{:S(2)}, u32[]{:S(2)}) collective-permute-start(bf16[2,16,16,256]{3,2,1,0:T(8,128)(2,1)S(1)} %get-tuple-element.75), channel_id=1, source_target_pairs={{64,0},{128,64},{192,128},{256,192},{320,256},{384,320},{448,384},... | collective-permute-start | bytes 786440 | tf_op jit(solution)/shard_map/ppermute | solution.py:27
  273.1 12.8 %collective-permute-start.6 = (bf16[4,1,16,256]{3,2,1,0:T(8,128)(2,1)S(1)}, bf16[4,1,16,256]{3,2,1,0:T(8,128)(2,1)S(1)}, u32[]{:S(2)}, u32[]{:S(2)}) collective-permute-start(bf16[4,1,16,256]{3,2,1,0:T(8,128)(2,1)S(1)} %get-tuple-element.73), channel_id=1, source_target_pairs={{0,16},{16,32},{32,48},{1,17},{17,33},{33,49},{2,18},{18,34},{34,5... | collective-permute-start | bytes 98312 | tf_op jit(solution)/shard_map/ppermute | solution.py:16
  277.7 8.3 %collective-permute-start.7 = (bf16[4,1,16,256]{3,2,1,0:T(8,128)(2,1)S(1)}, bf16[4,1,16,256]{3,2,1,0:T(8,128)(2,1)S(1)}, u32[]{:S(2)}, u32[]{:S(2)}) collective-permute-start(bf16[4,1,16,256]{3,2,1,0:T(8,128)(2,1)S(1)} %get-tuple-element.74), channel_id=1, source_target_pairs={{16,0},{32,16},{48,32},{17,1},{33,17},{49,33},{18,2},{34,18},{50,3... | collective-permute-start | bytes 98312 | tf_op jit(solution)/shard_map/ppermute | solution.py:19
  286.1 92.1 %collective-permute-start.8 = (bf16[4,18,1,256]{3,2,1,0:T(2,128)(2,1)S(1)}, bf16[4,18,1,256]{3,2,1,0:T(2,128)(2,1)S(1)}, u32[]{:S(2)}, u32[]{:S(2)}) collective-permute-start(bf16[4,18,1,256]{3,2,1,0:T(2,128)(2,1)S(1)} %get-tuple-element.54), channel_id=1, source_target_pairs={{0,1},{1,2},{2,3},{3,4},{4,5},{5,6},{6,7},{7,8},{8,9},{9,10},{10,1... | collective-permute-start | bytes 110600 | tf_op jit(solution)/shard_map/ppermute | solution.py:16
  376.2 5.7 %collective-permute-start.9 = (bf16[4,18,1,256]{3,2,1,0:T(2,128)(2,1)S(1)}, bf16[4,18,1,256]{3,2,1,0:T(2,128)(2,1)S(1)}, u32[]{:S(2)}, u32[]{:S(2)}) collective-permute-start(bf16[4,18,1,256]{3,2,1,0:T(2,128)(2,1)S(1)} %get-tuple-element.53), channel_id=1, source_target_pairs={{1,0},{2,1},{3,2},{4,3},{5,4},{6,5},{7,6},{8,7},{9,8},{10,9},{11,1... | collective-permute-start | bytes 110600 | tf_op jit(solution)/shard_map/ppermute | solution.py:19
  383.2 1.3 copy-start.4
  383.5 1.7 copy-start.1
Sparse Core Ops, SparseCore 0:
  58.7 187.8 all-gather.1
where the time goes:
time: 449 us; the launch traced here: 448 us
  waiting for transfers between devices  163 us (36%)
  starting transfers between devices  160 us (36%)
  other arithmetic  55.3 us (12%)
  local copies, waits for them, and re-layouts  40.2 us (9%)
  matrix products  14.6 us (3%)
  between operations  14.5 us (3%)
    ppermute x2, waiting for transfers between devices, from_behind(): lax.ppermute(value, axis, [(source, source + steps) for source in range(f...  109 us
    ppermute x4, starting transfers between devices, extended(): lax.ppermute(lax.slice_in_dim(block, block.shape[dim] - width, None, axis...  99.8 us
    scatter-add x1, other arithmetic, per_device(): crop_terms = jnp.zeros((frames * rows * cols, width), jnp.float32).at[cel...  44.7 us
    all_gather x1, waiting for transfers between devices, per_device(): gathered = lax.all_gather(conv_weight, 'wa', axis=0, tiled=True)  43.4 us
    ppermute x2, starting transfers between devices, from_behind(): lax.ppermute(value, axis, [(source, source + steps) for source in range(f...  21.7 us
    all_to_all x1, starting transfers between devices, per_device(): lax.all_to_all(meta_sent, ('ha', 'wa'), split_axis=0, concat_axis=0, tile...  16.4 us
    all_to_all x1, starting transfers between devices, per_device(): lax.all_to_all(packed, ('ha', 'wa'), split_axis=0, concat_axis=0, tiled=T...  13.4 us
    unnamed x32, local copies, waits for them, and re-layouts  11.2 us
  transfers between devices with their start and end apart: 13, of which 5 were waited for; matrix products, arithmetic and copies ran while one was open for 10% of the time, Pallas kernels for 0%

commit v1 on v0

--- a/solution.py
+++ b/solution.py
@@ -2,6 +2,7 @@
 import jax.numpy as jnp
 from jax import lax
 from jax.sharding import PartitionSpec as P
+from jax.lax import all_to_all, psum
 
 CH = 8
 CW = 8
@@ -103,7 +104,9 @@
         .at[cell_index.reshape(-1)]
         .add(received.reshape(-1, width).astype(jnp.float32))
     )
-    gathered = lax.all_gather(conv_weight, "wa", axis=0, tiled=True)
+    gathered = jnp.concatenate(
+        all_to_all(jnp.stack([conv_weight for _ in range(psum(1, "wa"))]), "wa", 0, 0), 0
+    )
     kernel_taps = gathered.reshape(27, width, width)
     past = from_behind(features, "ta", 1)
     padded = widen(jnp.concatenate([past, features], 0))

time: 449 us -> 541 us (1.20)
  waiting for transfers between devices: 163 us -> 222 us
  starting transfers between devices: 160 us -> 191 us
  blocking collectives: 0 us -> 28 us
  between operations: 14.5 us -> 1.21 us
    all_to_all x1, waiting for transfers between devices: 0.01 us -> 119 us  [per_device(): all_to_all(jnp.stack([conv_weight for _ in range(psum(1, 'wa'))]), 'wa',...]
    all_gather x1 -> x0, waiting for transfers between devices: 43.4 us -> none  [per_device(): gathered = lax.all_gather(conv_weight, 'wa', axis=0, tiled=True)]
    ppermute x4, starting transfers between devices: 99.8 us -> 131 us  [extended(): lax.ppermute(lax.slice_in_dim(block, block.shape[dim] - width, None, axis...]
    all_to_all x0 -> x1, blocking collectives: none -> 28 us  [per_device(): lax.all_to_all(meta_sent, ('ha', 'wa'), split_axis=0, concat_axis=0, tile...]
    all_to_all x1, starting transfers between devices: 13.4 us -> 31.5 us  [per_device(): lax.all_to_all(packed, ('ha', 'wa'), split_axis=0, concat_axis=0, tiled=T...]
    ppermute x2, waiting for transfers between devices: 109 us -> 93.7 us  [from_behind(): lax.ppermute(value, axis, [(source, source + steps) for source in range(f...]
    all_to_all x1, starting transfers between devices: 16.4 us -> 4.78 us  [per_device(): all_to_all(jnp.stack([conv_weight for _ in range(psum(1, 'wa'))]), 'wa',...]
    ppermute x2, starting transfers between devices: 21.7 us -> 14.3 us  [from_behind(): lax.ppermute(value, axis, [(source, source + steps) for source in range(f...]
  transfers between devices with their start and end apart: 13 -> 12, of which waited for: 5 -> 6; matrix products, arithmetic and copies ran while one was open for 10% -> 5% of each run, Pallas kernels for 0% -> 0%
where the time goes in v1:
time: 541 us; the launch traced here: 540 us
  waiting for transfers between devices  222 us (41%)
  starting transfers between devices  191 us (35%)
  other arithmetic  51.2 us (9%)
  local copies, waits for them, and re-layouts  37 us (7%)
  blocking collectives  28 us (5%)
  matrix products  9.22 us (2%)
    ppermute x4, starting transfers between devices, extended(): lax.ppermute(lax.slice_in_dim(block, block.shape[dim] - width, None, axis...  131 us
    all_to_all x1, waiting for transfers between devices, per_device(): all_to_all(jnp.stack([conv_weight for _ in range(psum(1, 'wa'))]), 'wa',...  119 us
    ppermute x2, waiting for transfers between devices, from_behind(): lax.ppermute(value, axis, [(source, source + steps) for source in range(f...  93.7 us
    scatter-add x1, other arithmetic, per_device(): crop_terms = jnp.zeros((frames * rows * cols, width), jnp.float32).at[cel...  44.7 us
    all_to_all x1, starting transfers between devices, per_device(): lax.all_to_all(packed, ('ha', 'wa'), split_axis=0, concat_axis=0, tiled=T...  31.5 us
    all_to_all x1, blocking collectives, per_device(): lax.all_to_all(meta_sent, ('ha', 'wa'), split_axis=0, concat_axis=0, tile...  28 us
    ppermute x2, starting transfers between devices, from_behind(): lax.ppermute(value, axis, [(source, source + steps) for source in range(f...  14.3 us
  transfers between devices with their start and end apart: 12, of which 6 were waited for; matrix products, arithmetic and copies ran while one was open for 5% of the time, Pallas kernels for 0%

profile of v1, /device:TPU:27, one launch (start us, length us, event | category | flops | bytes accessed | tf_op | source)
XLA Modules:
  0.0 540.4 jit_solution(17558299741106687546)
XLA Ops:
  0.6 0.8 fusion.19
  1.5 0.8 select_reduce_fusion
  2.4 0.7 fusion.21
  3.1 0.7 pad_add_fusion
  4.0 28.0 %all_to_all.26 = s32[64,2,3]{2,1,0:T(2,128)S(1)} all-to-all(s32[64,2,3]{2,1,0:T(2,128)S(1)} %bitcast.92), channel_id=1, replica_groups=mesh['ta'=8,'ha'=4,'wa'=16] {'ha','wa'}, dimensions={0} | all-to-all | bytes 3072 | tf_op jit(solution)/shard_map/all_to_all | solution.py:92
  32.1 2.9 stack.10
  35.0 4.8 all-to-all-start
  40.0 1.3 copy.92
  41.3 3.4 convolution_convert_fusion
  44.7 7.6 %all_to_all.21 = bf16[64,2,16384]{2,1,0:T(2,128)(2,1)} reshape(bf16[128,16384]{1,0:T(8,128)(2,1)} %convolution_convert_fusion) | data formatting | bytes 8388608 | tf_op jit(solution)/shard_map/all_to_all | solution.py:91
  52.3 119.1 %all-to-all-done = bf16[16,432,256]{2,1,0:T(8,128)(2,1)} async-done(((bf16[16,432,256]{2,1,0:T(8,128)(2,1)}), bf16[16,432,256]{2,1,0:T(8,128)(2,1)}, u32[]{:S(2)}, u32[]{:S(2)}) %all-to-all-start) | async-done | bytes 3538976 | tf_op jit(solution)/shard_map/all_to_all | solution.py:108
  171.3 31.5 %all-to-all-start.2 = ((bf16[64,2,16384]{2,1,0:T(2,128)(2,1)}), bf16[64,2,16384]{2,1,0:T(2,128)(2,1)}, u32[]{:S(2)}, u32[]{:S(2)}) async-start(bf16[64,2,16384]{2,1,0:T(2,128)(2,1)} %all_to_all.21), calls=%async_computation.2 | async-start | bytes 8388608 | tf_op jit(solution)/shard_map/all_to_all | solution.py:91
  202.9 7.9 %collective-permute-start = (bf16[2,16,16,256]{3,2,1,0:T(8,128)(2,1)S(1)}, bf16[2,16,16,256]{3,2,1,0:T(8,128)(2,1)S(1)}, u32[]{:S(2)}, u32[]{:S(2)}) collective-permute-start(bf16[2,16,16,256]{3,2,1,0:T(8,128)(2,1)S(1)} %copy-done.2), channel_id=1, source_target_pairs={{0,64},{64,128},{128,192},{192,256},{256,320},{320,384},{384,448},... | collective-permute-start | bytes 786440 | tf_op jit(solution)/shard_map/ppermute | solution.py:28
  211.2 0.4 copy.74
  212.0 87.6 %collective-permute-done = bf16[2,16,16,256]{3,2,1,0:T(8,128)(2,1)S(1)} collective-permute-done((bf16[2,16,16,256]{3,2,1,0:T(8,128)(2,1)S(1)}, bf16[2,16,16,256]{3,2,1,0:T(8,128)(2,1)S(1)}, u32[]{:S(2)}, u32[]{:S(2)}) %collective-permute-start) | collective-permute-done | bytes 262176 | tf_op jit(solution)/shard_map/ppermute | solution.py:28
  299.7 3.2 collective-permute-start.1
  302.9 2.1 collective-permute-start.2
  305.5 2.5 collective-permute-done.2
  308.1 1.9 collective-permute-start.3
  310.1 3.1 collective-permute-start.4
  313.3 3.4 collective-permute-done.4
  316.7 0.6 pad_maximum_fusion
  318.3 2.2 fusion.23
  320.5 0.8 fusion.26
  321.3 0.8 convolution_add_fusion.3
  322.1 0.8 convolution_add_fusion.2
  323.2 6.3 %collective-permute-start.5 = (bf16[2,16,16,256]{3,2,1,0:T(8,128)(2,1)S(1)}, bf16[2,16,16,256]{3,2,1,0:T(8,128)(2,1)S(1)}, u32[]{:S(2)}, u32[]{:S(2)}) collective-permute-start(bf16[2,16,16,256]{3,2,1,0:T(8,128)(2,1)S(1)} %get-tuple-element.78), channel_id=1, source_target_pairs={{64,0},{128,64},{192,128},{256,192},{320,256},{384,320},{448,384},... | collective-permute-start | bytes 786440 | tf_op jit(solution)/shard_map/ppermute | solution.py:28
  330.0 2.4 reverse_bitcast_fusion
  332.4 1.7 fusion.22
  334.1 6.1 %collective-permute-done.5 = bf16[2,16,16,256]{3,2,1,0:T(8,128)(2,1)S(1)} collective-permute-done((bf16[2,16,16,256]{3,2,1,0:T(8,128)(2,1)S(1)}, bf16[2,16,16,256]{3,2,1,0:T(8,128)(2,1)S(1)}, u32[]{:S(2)}, u32[]{:S(2)}) %collective-permute-start.5) | collective-permute-done | bytes 262176 | tf_op jit(solution)/shard_map/ppermute | solution.py:28
  340.2 2.9 collective-permute-start.6
  343.2 2.4 collective-permute-start.7
  345.5 0.9 convolution_convert_fusion.1
  346.4 2.4 copy.76
  348.8 1.5 copy.77
  350.4 1.6 copy.78
  352.1 123.2 %collective-permute-start.8 = (bf16[4,18,1,256]{3,2,1,0:T(2,128)(2,1)S(1)}, bf16[4,18,1,256]{3,2,1,0:T(2,128)(2,1)S(1)}, u32[]{:S(2)}, u32[]{:S(2)}) collective-permute-start(bf16[4,18,1,256]{3,2,1,0:T(2,128)(2,1)S(1)} %get-tuple-element.57), channel_id=1, source_target_pairs={{0,1},{1,2},{2,3},{3,4},{4,5},{5,6},{6,7},{7,8},{8,9},{9,10},{10,1... | collective-permute-start | bytes 110600 | tf_op jit(solution)/shard_map/ppermute | solution.py:17
  475.3 1.9 collective-permute-start.9
  477.3 3.6 collective-permute-done.9
  481.0 0.6 pad_maximum_fusion.1
  482.6 0.9 copy-done.4
  483.5 0.8 fusion.27
  484.3 0.8 convolution_add_fusion.1
  485.1 0.8 convolution_add_fusion
  485.9 8.2 %reshape.229 = f32[8192,256]{1,0:T(8,128)} reshape(bf16[64,2,16384]{2,1,0:T(2,128)(2,1)} %all-to-all-done.2) | data formatting | bytes 12582912 | tf_op jit(solution)/shard_map/convert_element_type | solution.py:105
  494.1 44.7 %scatter_custom_fusion = f32[512,256]{1,0:T(8,128)S(1)} fusion(s32[8192]{0:T(1024)S(1)} %bitcast.94, f32[8192,256]{1,0:T(8,128)} %reshape.229, f32[]{:T(128)} %constant.7.clone.1), kind=kCustom, calls=%fused_computation.92 | custom fusion | flops 2097152 | bytes 524800 | tf_op jit(solution)/shard_map/scatter-add | solution.py:105
  538.8 0.9 fusion.1
  539.7 0.7 copy.84
  (66 shorter events, 5.0 us)
Async XLA Ops:
  0.6 210.2 %copy-start = (bf16[2,2,256,256]{3,2,1,0:T(8,128)(2,1)S(1)}, bf16[2,2,256,256]{3,2,1,0:T(8,128)(2,1)}, u32[]{:S(2)}) copy-start(bf16[2,2,256,256]{3,2,1,0:T(8,128)(2,1)} %param.12) | copy-start | bytes 1572868
  35.0 4.8 copy-start.6
  35.0 4.8 copy-start.3
  35.0 136.4 %all-to-all-start = ((bf16[16,432,256]{2,1,0:T(8,128)(2,1)}), bf16[16,432,256]{2,1,0:T(8,128)(2,1)}, u32[]{:S(2)}, u32[]{:S(2)}) async-start(bf16[16,432,256]{2,1,0:T(8,128)(2,1)} %stack.10), calls=%async_computation | async-start | bytes 7077888 | tf_op jit(solution)/shard_map/all_to_all | solution.py:108
  52.3 150.6 %copy-start.2 = (bf16[2,16,16,256]{3,2,1,0:T(8,128)(2,1)S(1)}, bf16[2,16,16,256]{3,2,1,0:T(8,128)(2,1)}, u32[]{:S(2)}) copy-start(bf16[2,16,16,256]{3,2,1,0:T(8,128)(2,1)} %param.10) | copy-start | bytes 786436
  52.3 158.6 %copy-start.5 = (bf16[2,8,8,256]{3,2,1,0:T(8,128)(2,1)S(1)}, bf16[2,8,8,256]{3,2,1,0:T(8,128)(2,1)}, u32[]{:S(2)}) copy-start(bf16[2,8,8,256]{3,2,1,0:T(8,128)(2,1)} %param.13) | copy-start | bytes 196612
  171.3 314.6 %all-to-all-start.2 = ((bf16[64,2,16384]{2,1,0:T(2,128)(2,1)}), bf16[64,2,16384]{2,1,0:T(2,128)(2,1)}, u32[]{:S(2)}, u32[]{:S(2)}) async-start(bf16[64,2,16384]{2,1,0:T(2,128)(2,1)} %all_to_all.21), calls=%async_computation.2 | async-start | bytes 8388608 | tf_op jit(solution)/shard_map/all_to_all | solution.py:91
  202.9 96.8 %collective-permute-start = (bf16[2,16,16,256]{3,2,1,0:T(8,128)(2,1)S(1)}, bf16[2,16,16,256]{3,2,1,0:T(8,128)(2,1)S(1)}, u32[]{:S(2)}, u32[]{:S(2)}) collective-permute-start(bf16[2,16,16,256]{3,2,1,0:T(8,128)(2,1)S(1)} %copy-done.2), channel_id=1, source_target_pairs={{0,64},{64,128},{128,192},{192,256},{256,320},{320,384},{384,448},... | collective-permute-start | bytes 786440 | tf_op jit(solution)/shard_map/ppermute | solution.py:28
  299.7 5.8 %collective-permute-start.1 = (bf16[4,1,16,256]{3,2,1,0:T(8,128)(2,1)S(1)}, bf16[4,1,16,256]{3,2,1,0:T(8,128)(2,1)S(1)}, u32[]{:S(2)}, u32[]{:S(2)}) collective-permute-start(bf16[4,1,16,256]{3,2,1,0:T(8,128)(2,1)S(1)} %get-tuple-element.80), channel_id=1, source_target_pairs={{0,16},{16,32},{32,48},{1,17},{17,33},{33,49},{2,18},{18,34},{34,5... | collective-permute-start | bytes 98312 | tf_op jit(solution)/shard_map/ppermute | solution.py:17
  302.9 5.1 collective-permute-start.2
  308.1 5.1 collective-permute-start.3
  310.1 6.6 %collective-permute-start.4 = (bf16[4,18,1,256]{3,2,1,0:T(2,128)(2,1)S(1)}, bf16[4,18,1,256]{3,2,1,0:T(2,128)(2,1)S(1)}, u32[]{:S(2)}, u32[]{:S(2)}) collective-permute-start(bf16[4,18,1,256]{3,2,1,0:T(2,128)(2,1)S(1)} %get-tuple-element.60), channel_id=1, source_target_pairs={{1,0},{2,1},{3,2},{4,3},{5,4},{6,5},{7,6},{8,7},{9,8},{10,9},{11,1... | collective-permute-start | bytes 110600 | tf_op jit(solution)/shard_map/ppermute | solution.py:20
  323.2 17.1 %collective-permute-start.5 = (bf16[2,16,16,256]{3,2,1,0:T(8,128)(2,1)S(1)}, bf16[2,16,16,256]{3,2,1,0:T(8,128)(2,1)S(1)}, u32[]{:S(2)}, u32[]{:S(2)}) collective-permute-start(bf16[2,16,16,256]{3,2,1,0:T(8,128)(2,1)S(1)} %get-tuple-element.78), channel_id=1, source_target_pairs={{64,0},{128,64},{192,128},{256,192},{320,256},{384,320},{448,384},... | collective-permute-start | bytes 786440 | tf_op jit(solution)/shard_map/ppermute | solution.py:28
  340.2 11.7 %collective-permute-start.6 = (bf16[4,1,16,256]{3,2,1,0:T(8,128)(2,1)S(1)}, bf16[4,1,16,256]{3,2,1,0:T(8,128)(2,1)S(1)}, u32[]{:S(2)}, u32[]{:S(2)}) collective-permute-start(bf16[4,1,16,256]{3,2,1,0:T(8,128)(2,1)S(1)} %get-tuple-element.76), channel_id=1, source_target_pairs={{0,16},{16,32},{32,48},{1,17},{17,33},{33,49},{2,18},{18,34},{34,5... | collective-permute-start | bytes 98312 | tf_op jit(solution)/shard_map/ppermute | solution.py:17
  343.2 8.8 %collective-permute-start.7 = (bf16[4,1,16,256]{3,2,1,0:T(8,128)(2,1)S(1)}, bf16[4,1,16,256]{3,2,1,0:T(8,128)(2,1)S(1)}, u32[]{:S(2)}, u32[]{:S(2)}) collective-permute-start(bf16[4,1,16,256]{3,2,1,0:T(8,128)(2,1)S(1)} %get-tuple-element.77), channel_id=1, source_target_pairs={{16,0},{32,16},{48,32},{17,1},{33,17},{49,33},{18,2},{34,18},{50,3... | collective-permute-start | bytes 98312 | tf_op jit(solution)/shard_map/ppermute | solution.py:20
  352.1 125.3 %collective-permute-start.8 = (bf16[4,18,1,256]{3,2,1,0:T(2,128)(2,1)S(1)}, bf16[4,18,1,256]{3,2,1,0:T(2,128)(2,1)S(1)}, u32[]{:S(2)}, u32[]{:S(2)}) collective-permute-start(bf16[4,18,1,256]{3,2,1,0:T(2,128)(2,1)S(1)} %get-tuple-element.57), channel_id=1, source_target_pairs={{0,1},{1,2},{2,3},{3,4},{4,5},{5,6},{6,7},{7,8},{8,9},{9,10},{10,1... | collective-permute-start | bytes 110600 | tf_op jit(solution)/shard_map/ppermute | solution.py:17
  475.3 5.7 %collective-permute-start.9 = (bf16[4,18,1,256]{3,2,1,0:T(2,128)(2,1)S(1)}, bf16[4,18,1,256]{3,2,1,0:T(2,128)(2,1)S(1)}, u32[]{:S(2)}, u32[]{:S(2)}) collective-permute-start(bf16[4,18,1,256]{3,2,1,0:T(2,128)(2,1)S(1)} %get-tuple-element.56), channel_id=1, source_target_pairs={{1,0},{2,1},{3,2},{4,3},{5,4},{6,5},{7,6},{8,7},{9,8},{10,9},{11,1... | collective-permute-start | bytes 110600 | tf_op jit(solution)/shard_map/ppermute | solution.py:20
  482.3 1.3 copy-start.4
  482.6 1.7 copy-start.1
